TPU v7x, 256 devices: a whole 4x4x8 slice. The times are simulated.
256 devices in a mesh: tok: 16 (over y, x), col: 16 (over z, core).
Axes of the slice: x: 4, y: 4, z: 8, core: 2. Of those that a mesh axis runs over, the one named last changes fastest.
Arguments:
- activations: bfloat16 [32768, 8192], P('tok', 'col'), may hold values from -60 to 60, as said below
- weight: bfloat16 [8192, 8192], P('tok', 'col'), may hold values from -6 to 6
- keep_mask: int32 [8192, 8192], P('tok', 'col'), may hold values from 0 to 1
Outputs:
- new_weight: bfloat16 [8192, 8192], P('tok', 'col')
Inputs may be any that keep to these rules, and one draw needn't show every extreme that they name: activations of calibration tokens.
All inputs are finite; a program needn't handle non-finite values.
Results may differ from a plain program's by a relative error of at most 0.00115.
Values may be sent and summed in bfloat16 or wider, within the bound.
A program may use at most 64 MiB of HBM per device.

v0:
```python
import jax
import jax.numpy as jnp
from jax import lax
from jax.sharding import PartitionSpec as P

B = 1024
ITERS = 4


def split(x):
    high = lax.reduce_precision(x, exponent_bits=8, mantissa_bits=7)
    return (high.astype(jnp.bfloat16), (x - high).astype(jnp.bfloat16))


def mm(a, b, dims=(((1,), (0,)), ((), ()))):
    return lax.dot_general(a, b, dims, preferred_element_type=jnp.float32)


def per_device(activations, weight, keep_mask):
    n_col = lax.axis_size("col")
    n_tok = lax.axis_size("tok")
    tok_rows = activations.shape[0]
    panel_width = B // n_col
    total_count = tok_rows * n_tok
    pruned = jnp.where(
        keep_mask[:, :panel_width] == 0, weight[:, :panel_width], jnp.zeros((), jnp.bfloat16)
    )
    panel = lax.all_gather(activations[:, :panel_width], "col", axis=1, tiled=True)
    partial_panel = mm(activations, panel, (((0,), (0,)), ((), ())))
    pruned_panel = lax.all_gather(pruned, "col", axis=1, tiled=True)
    hessian_panel = lax.psum(partial_panel, "tok") / total_count
    block = lax.all_gather(hessian_panel[:panel_width], "col", axis=0, tiled=True)
    rows = lax.broadcasted_iota(jnp.int32, (B, B), 0)
    columns = lax.broadcasted_iota(jnp.int32, (B, B), 1)
    on_diagonal = rows == columns
    mean_diagonal = jnp.sum(jnp.where(on_diagonal, block, 0.0)) / B
    damped = block + jnp.where(on_diagonal, 0.01 * mean_diagonal, 0.0)
    scale = lax.rsqrt(jnp.sum(damped * damped))
    g = damped * scale
    y = pruned_panel.astype(jnp.float32)
    for sweep in range(ITERS):
        g_high = g.astype(jnp.bfloat16)
        y_high, y_low = split(y)
        y = 2.0 * y - (mm(y_high, g_high) + mm(y_low, g_high))
        if sweep < ITERS - 1:
            g = 2.0 * g - mm(g_high, g_high)
    y_high, y_low = split(y * scale)
    h_high, h_low = split(hessian_panel)
    nt = (((1,), (1,)), ((), ()))
    correction = mm(y_high, h_high, nt) + mm(y_low, h_high, nt) + mm(y_high, h_low, nt)
    kept = keep_mask.astype(jnp.float32)
    return (kept * (weight.astype(jnp.float32) - correction)).astype(jnp.bfloat16)


def solution(mesh):
    return jax.shard_map(
        per_device,
        mesh=mesh,
        in_specs=(P("tok", "col"), P("tok", "col"), P("tok", "col")),
        out_specs=P("tok", "col"),
        check_vma=False,
    )
```

profile of v0, /device:TPU:1, one launch (start us, length us, event | category | flops | bytes accessed | tf_op | source)
XLA Modules:
  0.0 284.6 jit_solution(3406045359667828655)
XLA Ops:
  6.5 1.2 slice.14
  7.8 0.9 copy.10
  8.7 46.8 %all-gather.6.cloned.1.call-done = bf16[2048,1024]{0,1:T(8,128)(2,1)} async-done(((bf16[2048,64]{0,1:T(8,128)(2,1)}), bf16[2048,1024]{0,1:T(8,128)(2,1)}) %all-gather.6.cloned.1.call-update) | async-done | bytes 4194320 | tf_op jit(solution)/shard_map/all_gather | solution.py:28
  55.6 5.9 %fusion.29 = f32[512,1024]{1,0:T(8,128)} fusion(bf16[2048,512]{1,0:T(8,128)(2,1)S(1)} %copy-done.4, bf16[2048,1024]{0,1:T(8,128)(2,1)} %all-gather.6.cloned.1.call-done), kind=kOutput, calls=%fused_computation.50 | convolution fusion | flops 2147483648 | bytes 8388608 | tf_op jit(solution)/shard_map/dot_general | solution.py:16
  61.5 0.8 slice-done.1
  63.3 95.8 %all-reduce.2.cloned.1.call-done = f32[512,1024]{1,0:T(8,128)} async-done(((f32[512,1024]{1,0:T(8,128)}), f32[512,1024]{1,0:T(8,128)}) %all-reduce.2.cloned.1.call-update) | async-done | bytes 2097168 | tf_op jit(solution)/shard_map/psum | solution.py:31
  159.1 1.8 broadcast_multiply_fusion
  161.6 39.0 %all-gather.4.cloned.1.call-done = bf16[512,1024]{0,1:T(8,128)(2,1)} async-done(((bf16[512,64]{0,1:T(8,128)(2,1)}), bf16[512,1024]{0,1:T(8,128)(2,1)}) %all-gather.4.cloned.1.call-update) | async-done | bytes 1048592 | tf_op jit(solution)/shard_map/all_gather | solution.py:30
  200.6 1.7 copy.6
  202.3 41.0 %all-gather.8.cloned.1.call-done = f32[1024,1024]{1,0:T(8,128)} async-done(((f32[64,1024]{1,0:T(8,128)}), f32[1024,1024]{1,0:T(8,128)}) %all-gather.8.cloned.1.call-update) | async-done | bytes 4194320 | tf_op jit(solution)/shard_map/all_gather | solution.py:32
  243.3 2.9 %select_reduce_fusion = f32[]{:T(128)} fusion(f32[1024,1024]{1,0:T(8,128)} %all-gather.8.cloned.1.call-done), kind=kLoop, calls=%fused_computation.5 | loop fusion | flops 3145727 | bytes 4194308 | tf_op jit(solution)/shard_map/reduce_sum | solution.py:36
  246.9 3.9 %multiply_reduce_fusion = f32[]{:T(128)} fusion(f32[1024,1024]{1,0:T(8,128)} %all-gather.8.cloned.1.call-done, f32[]{:T(128)S(6)} %mul_shard_map.3), kind=kLoop, calls=%fused_computation.3 | loop fusion | flops 5242879 | bytes 4194312 | tf_op jit(solution)/shard_map/reduce_sum | solution.py:38
  251.4 7.0 %multiply_subtract_fusion.1 = f32[1024,1024]{1,0:T(8,128)S(1)} fusion(f32[1024,1024]{1,0:T(8,128)} %all-gather.8.cloned.1.call-done, f32[]{:T(128)S(6)} %rsqrt.3, f32[]{:T(128)S(6)} %mul_shard_map.3), kind=kOutput, calls=%fused_computation.2 | convolution fusion | flops 2159017984 | bytes 8388616 | tf_op jit(solution)/shard_map/dot_general | solution.py:16
  258.5 2.3 multiply_subtract_fusion
  260.8 1.3 fusion.20
  262.1 1.4 fusion.6
  263.5 1.3 fusion.17
  264.8 1.3 add_subtract_fusion.1
  266.2 2.4 subtract_convert_fusion
  268.5 1.3 fusion.18
  269.8 1.6 add_subtract_fusion
  271.5 1.3 fusion.19
  272.7 1.4 subtract_multiply_fusion
  276.4 1.6 fusion.10
  (27 shorter events, 4.1 us)
Async XLA Ops:
  6.5 49.0 %copy-start.4 = (bf16[2048,512]{1,0:T(8,128)(2,1)S(1)}, bf16[2048,512]{1,0:T(8,128)(2,1)}, u32[]{:S(2)}) copy-start(bf16[2048,512]{1,0:T(8,128)(2,1)} %param.3) | copy-start | bytes 6291460
  6.5 49.0 %all-gather.6.cloned.1.call-start = ((), (), s32[]{:S(2)}) async-start(), calls=%async_computation.1 | async-start | bytes 4456448 | tf_op jit(solution)/shard_map/all_gather | solution.py:28
  8.7 150.4 %all-reduce.2.cloned.1.call-start = ((), (), s32[]{:S(2)}) async-start(), calls=%async_computation.2 | async-start | bytes 4194304 | tf_op jit(solution)/shard_map/psum | solution.py:31
  61.5 0.9 slice-start.1
  61.5 1.0 slice-start
  61.5 139.1 %all-gather.4.cloned.1.call-start = ((), (), s32[]{:S(2)}) async-start(), calls=%async_computation | async-start | bytes 1114112 | tf_op jit(solution)/shard_map/all_gather | solution.py:30
  63.3 180.0 %all-gather.8.cloned.1.call-start = ((), (), s32[]{:S(2)}) async-start(), calls=%async_computation.3 | async-start | bytes 4456448 | tf_op jit(solution)/shard_map/all_gather | solution.py:32
  258.5 2.4 copy-start.1
  272.7 1.6 copy-start
  275.1 1.2 copy-start.2
  275.1 1.3 copy-start.3
Sparse Core Ops, SparseCore 0:
  9.2 46.3 all-gather.5
  61.6 97.4 all-reduce.1
  161.1 39.5 all-gather.3
  202.4 40.7 all-gather.7
where the time goes:
time: 285 us
  waiting for transfers between devices  223 us (78%)
  matrix products  31.6 us (11%)
  between operations  14.6 us (5%)
  other arithmetic  9.21 us (3%)
  local copies, waits for them, and re-layouts  6.38 us (2%)
    psum x1, waiting for transfers between devices, per_device(): hessian_panel = lax.psum(partial_panel, 'tok') / total_count  95.8 us
    all_gather x1, waiting for transfers between devices, per_device(): lax.all_gather(activations[:, :panel_width], 'col', axis=1, tiled=True)  46.8 us
    all_gather x1, waiting for transfers between devices, per_device(): lax.all_gather(hessian_panel[:panel_width], 'col', axis=0, tiled=True)  41 us
    all_gather x1, waiting for transfers between devices, per_device(): pruned_panel = lax.all_gather(pruned, 'col', axis=1, tiled=True)  39 us
    dot_general x15, matrix products, mm(): return lax.dot_general(a, b, dims, preferred_element_type=jnp.float32)  31.6 us
  transfers between devices with their start and end apart: 4, of which 4 were waited for; matrix products, arithmetic and copies ran while one was open for 2% of the time, Pallas kernels for 0%

commit v1 on v0

--- a/solution.py
+++ b/solution.py
@@ -27,7 +27,18 @@
     )
     panel = lax.all_gather(activations[:, :panel_width], "col", axis=1, tiled=True)
     partial_panel = mm(activations, panel, (((0,), (0,)), ((), ())))
-    pruned_panel = lax.all_gather(pruned, "col", axis=1, tiled=True)
+    n_slots = lax.axis_size("col")
+    shelf = [(p, (p + 1) % n_slots) for p in range(n_slots)]
+    entries = [(p, (p - 1) % n_slots) for p in range(n_slots)]
+    last, reached = ([pruned], [pruned])
+    for _ in range(n_slots // 2):
+        k_now = lax.ppermute(last[-1], "col", shelf)
+        last.append(k_now)
+    for _ in tuple(range((n_slots - 1) // 2)):
+        wide_out = lax.ppermute(reached[-1], "col", entries)
+        reached.append(wide_out)
+    tall = jnp.concatenate([*last[::-1], *reached[1:]], axis=1)
+    pruned_panel = jnp.roll(tall, (lax.axis_index("col") - n_slots // 2) * pruned.shape[1], axis=1)
     hessian_panel = lax.psum(partial_panel, "tok") / total_count
     block = lax.all_gather(hessian_panel[:panel_width], "col", axis=0, tiled=True)
     rows = lax.broadcasted_iota(jnp.int32, (B, B), 0)

time: 285 us -> 264 us (0.926)
  the two profiles are of different devices: /device:TPU:1 before, /device:TPU:6 now
where the time goes in v1:
time: 264 us
  waiting for transfers between devices  174 us (66%)
  matrix products  31.7 us (12%)
  starting transfers between devices  23.2 us (9%)
  between operations  14.7 us (6%)
  local copies, waits for them, and re-layouts  10.3 us (4%)
  other arithmetic  9.52 us (4%)
    psum x1, waiting for transfers between devices, per_device(): hessian_panel = lax.psum(partial_panel, 'tok') / total_count  98.8 us
    all_gather x1, waiting for transfers between devices, per_device(): lax.all_gather(activations[:, :panel_width], 'col', axis=1, tiled=True)  45.5 us
    dot_general x15, matrix products, mm(): return lax.dot_general(a, b, dims, preferred_element_type=jnp.float32)  31.7 us
    ppermute x7, starting transfers between devices, per_device(): wide_out = lax.ppermute(reached[-1], 'col', entries)  23 us
    ppermute x7, waiting for transfers between devices, per_device(): wide_out = lax.ppermute(reached[-1], 'col', entries)  19.4 us
    ppermute x8, waiting for transfers between devices, per_device(): k_now = lax.ppermute(last[-1], 'col', shelf)  10.4 us
    concatenate x1, local copies, waits for them, and re-layouts, per_device(): jnp.roll(tall, (lax.axis_index('col') - n_slots // 2) * pruned.shape[1],...  6.23 us
  transfers between devices with their start and end apart: 18, of which 13 were waited for; matrix products, arithmetic and copies ran while one was open for 3% of the time, Pallas kernels for 0%

profile of v1, /device:TPU:6, one launch (start us, length us, event | category | flops | bytes accessed | tf_op | source)
XLA Modules:
  0.0 263.6 jit_solution(15248305475299800622)
XLA Ops:
  8.7 45.5 %all-gather.3.cloned.1.call-done = bf16[2048,1024]{0,1:T(8,128)(2,1)} async-done(((bf16[2048,64]{0,1:T(8,128)(2,1)}), bf16[2048,1024]{0,1:T(8,128)(2,1)}) %all-gather.3.cloned.1.call-update) | async-done | bytes 4194320 | tf_op jit(solution)/shard_map/all_gather | solution.py:28
  54.2 6.0 %fusion.34 = f32[512,1024]{1,0:T(8,128)} fusion(bf16[2048,512]{1,0:T(8,128)(2,1)S(1)} %copy-done.16, bf16[2048,1024]{0,1:T(8,128)(2,1)} %all-gather.3.cloned.1.call-done), kind=kOutput, calls=%fused_computation.55 | convolution fusion | flops 2147483648 | bytes 8388608 | tf_op jit(solution)/shard_map/dot_general | solution.py:16
  60.3 98.8 %all-reduce.2.cloned.1.call-done = f32[512,1024]{1,0:T(8,128)} async-done(((f32[512,1024]{1,0:T(8,128)}), f32[512,1024]{1,0:T(8,128)}) %all-reduce.2.cloned.1.call-update) | async-done | bytes 2097168 | tf_op jit(solution)/shard_map/psum | solution.py:42
  162.5 2.9 %collective-permute-start.8 = (bf16[512,64]{1,0:T(8,128)(2,1)S(1)}, bf16[512,64]{1,0:T(8,128)(2,1)S(1)}, u32[]{:S(2)}, u32[]{:S(2)}) collective-permute-start(bf16[512,64]{1,0:T(8,128)(2,1)S(1)} %fusion.25), channel_id=1, source_target_pairs={{0,15},{1,0},{2,1},{3,2},{4,3},{5,4},{6,5},{7,6},{8,7},{9,8},{10,9... | collective-permute-start | bytes 196616 | tf_op jit(solution)/shard_map/ppermute | solution.py:38
  165.5 2.6 %collective-permute-done = bf16[512,64]{1,0:T(8,128)(2,1)S(1)} collective-permute-done((bf16[512,64]{1,0:T(8,128)(2,1)S(1)}, bf16[512,64]{1,0:T(8,128)(2,1)S(1)}, u32[]{:S(2)}, u32[]{:S(2)}) %collective-permute-start) | collective-permute-done | bytes 65568 | tf_op jit(solution)/shard_map/ppermute | solution.py:35
  168.1 3.0 %collective-permute-start.9 = (bf16[512,64]{1,0:T(8,128)(2,1)S(1)}, bf16[512,64]{1,0:T(8,128)(2,1)S(1)}, u32[]{:S(2)}, u32[]{:S(2)}) collective-permute-start(bf16[512,64]{1,0:T(8,128)(2,1)S(1)} %collective-permute-done.8), channel_id=1, source_target_pairs={{0,15},{1,0},{2,1},{3,2},{4,3},{5,4},{6,5},{7,6},{8,7},{9,8},{10,9... | collective-permute-start | bytes 196616 | tf_op jit(solution)/shard_map/ppermute | solution.py:38
  171.1 2.6 %collective-permute-done.1 = bf16[512,64]{1,0:T(8,128)(2,1)S(1)} collective-permute-done((bf16[512,64]{1,0:T(8,128)(2,1)S(1)}, bf16[512,64]{1,0:T(8,128)(2,1)S(1)}, u32[]{:S(2)}, u32[]{:S(2)}) %collective-permute-start.1) | collective-permute-done | bytes 65568 | tf_op jit(solution)/shard_map/ppermute | solution.py:35
  175.8 3.5 %collective-permute-start.10 = (bf16[512,64]{1,0:T(8,128)(2,1)S(1)}, bf16[512,64]{1,0:T(8,128)(2,1)S(1)}, u32[]{:S(2)}, u32[]{:S(2)}) collective-permute-start(bf16[512,64]{1,0:T(8,128)(2,1)S(1)} %collective-permute-done.9), channel_id=1, source_target_pairs={{0,15},{1,0},{2,1},{3,2},{4,3},{5,4},{6,5},{7,6},{8,7},{9,8},{10,9... | collective-permute-start | bytes 196616 | tf_op jit(solution)/shard_map/ppermute | solution.py:38
  181.4 2.8 %collective-permute-done.10 = bf16[512,64]{1,0:T(8,128)(2,1)S(1)} collective-permute-done((bf16[512,64]{1,0:T(8,128)(2,1)S(1)}, bf16[512,64]{1,0:T(8,128)(2,1)S(1)}, u32[]{:S(2)}, u32[]{:S(2)}) %collective-permute-start.10) | collective-permute-done | bytes 65568 | tf_op jit(solution)/shard_map/ppermute | solution.py:38
  184.2 3.5 %collective-permute-start.11 = (bf16[512,64]{1,0:T(8,128)(2,1)S(1)}, bf16[512,64]{1,0:T(8,128)(2,1)S(1)}, u32[]{:S(2)}, u32[]{:S(2)}) collective-permute-start(bf16[512,64]{1,0:T(8,128)(2,1)S(1)} %collective-permute-done.10), channel_id=1, source_target_pairs={{0,15},{1,0},{2,1},{3,2},{4,3},{5,4},{6,5},{7,6},{8,7},{9,8},{10,9... | collective-permute-start | bytes 196616 | tf_op jit(solution)/shard_map/ppermute | solution.py:38
  188.2 4.6 %collective-permute-done.11 = bf16[512,64]{1,0:T(8,128)(2,1)S(1)} collective-permute-done((bf16[512,64]{1,0:T(8,128)(2,1)S(1)}, bf16[512,64]{1,0:T(8,128)(2,1)S(1)}, u32[]{:S(2)}, u32[]{:S(2)}) %collective-permute-start.11) | collective-permute-done | bytes 65568 | tf_op jit(solution)/shard_map/ppermute | solution.py:38
  192.9 3.5 %collective-permute-start.12 = (bf16[512,64]{1,0:T(8,128)(2,1)S(1)}, bf16[512,64]{1,0:T(8,128)(2,1)S(1)}, u32[]{:S(2)}, u32[]{:S(2)}) collective-permute-start(bf16[512,64]{1,0:T(8,128)(2,1)S(1)} %collective-permute-done.11), channel_id=1, source_target_pairs={{0,15},{1,0},{2,1},{3,2},{4,3},{5,4},{6,5},{7,6},{8,7},{9,8},{10,9... | collective-permute-start | bytes 196616 | tf_op jit(solution)/shard_map/ppermute | solution.py:38
  196.4 5.0 %collective-permute-done.12 = bf16[512,64]{1,0:T(8,128)(2,1)S(1)} collective-permute-done((bf16[512,64]{1,0:T(8,128)(2,1)S(1)}, bf16[512,64]{1,0:T(8,128)(2,1)S(1)}, u32[]{:S(2)}, u32[]{:S(2)}) %collective-permute-start.12) | collective-permute-done | bytes 65568 | tf_op jit(solution)/shard_map/ppermute | solution.py:38
  201.4 3.5 %collective-permute-start.13 = (bf16[512,64]{1,0:T(8,128)(2,1)S(1)}, bf16[512,64]{1,0:T(8,128)(2,1)S(1)}, u32[]{:S(2)}, u32[]{:S(2)}) collective-permute-start(bf16[512,64]{1,0:T(8,128)(2,1)S(1)} %collective-permute-done.12), channel_id=1, source_target_pairs={{0,15},{1,0},{2,1},{3,2},{4,3},{5,4},{6,5},{7,6},{8,7},{9,8},{10,9... | collective-permute-start | bytes 196616 | tf_op jit(solution)/shard_map/ppermute | solution.py:38
  204.9 2.5 collective-permute-done.13
  207.4 3.1 %collective-permute-start.14 = (bf16[512,64]{1,0:T(8,128)(2,1)S(1)}, bf16[512,64]{1,0:T(8,128)(2,1)S(1)}, u32[]{:S(2)}, u32[]{:S(2)}) collective-permute-start(bf16[512,64]{1,0:T(8,128)(2,1)S(1)} %collective-permute-done.13), channel_id=1, source_target_pairs={{0,15},{1,0},{2,1},{3,2},{4,3},{5,4},{6,5},{7,6},{8,7},{9,8},{10,9... | collective-permute-start | bytes 196616 | tf_op jit(solution)/shard_map/ppermute | solution.py:38
  210.5 2.5 collective-permute-done.14
  213.7 2.5 collective-permute-done.7
  216.2 6.2 %concatenate.6 = bf16[512,2048]{1,0:T(8,128)(2,1)S(1)} concatenate(bf16[512,64]{1,0:T(8,128)(2,1)} %collective-permute-done.7, bf16[512,64]{1,0:T(8,128)(2,1)} %copy-done.14, bf16[512,64]{1,0:T(8,128)(2,1)} %copy-done.12, bf16[512,64]{1,0:T(8,128)(2,1)} %copy-done.10, bf16[512,64]{1,0:T(8,128)(2,1)} %copy-done.8, bf16[512,64]{1,0:T(8,128)(2,1)} %copy-done.6, ...), dimensions={1} | concatenate | bytes 4194304 | tf_op jit(solution)/shard_map/jit(_roll_dynamic)/concatenate | solution.py:41
  222.5 2.9 %select_reduce_fusion = f32[]{:T(128)} fusion(f32[1024,1024]{1,0:T(8,128)} %all-gather.5.cloned.1.call-done), kind=kLoop, calls=%fused_computation.5 | loop fusion | flops 3145727 | bytes 4194308 | tf_op jit(solution)/shard_map/reduce_sum | solution.py:47
  226.1 3.9 %multiply_reduce_fusion = f32[]{:T(128)} fusion(f32[1024,1024]{1,0:T(8,128)} %all-gather.5.cloned.1.call-done, f32[]{:T(128)S(6)} %mul_shard_map.3), kind=kLoop, calls=%fused_computation.3 | loop fusion | flops 5242879 | bytes 4194312 | tf_op jit(solution)/shard_map/reduce_sum | solution.py:49
  230.6 7.1 %multiply_subtract_fusion.1 = f32[1024,1024]{1,0:T(8,128)S(1)} fusion(f32[1024,1024]{1,0:T(8,128)} %all-gather.5.cloned.1.call-done, f32[]{:T(128)S(6)} %rsqrt.3, f32[]{:T(128)S(6)} %mul_shard_map.3), kind=kOutput, calls=%fused_computation.2 | convolution fusion | flops 2159017984 | bytes 8388616 | tf_op jit(solution)/shard_map/dot_general | solution.py:16
  237.8 2.4 multiply_subtract_fusion
  245.6 2.4 subtract_convert_fusion
  (72 shorter events, 25.6 us)
Async XLA Ops:
  6.5 47.7 %copy-start.16 = (bf16[2048,512]{1,0:T(8,128)(2,1)S(1)}, bf16[2048,512]{1,0:T(8,128)(2,1)}, u32[]{:S(2)}) copy-start(bf16[2048,512]{1,0:T(8,128)(2,1)} %param.3) | copy-start | bytes 6291460
  6.5 47.7 %all-gather.3.cloned.1.call-start = ((), (), s32[]{:S(2)}) async-start(), calls=%async_computation | async-start | bytes 4456448 | tf_op jit(solution)/shard_map/all_gather | solution.py:28
  8.7 150.4 %all-reduce.2.cloned.1.call-start = ((), (), s32[]{:S(2)}) async-start(), calls=%async_computation.1 | async-start | bytes 4194304 | tf_op jit(solution)/shard_map/psum | solution.py:42
  60.2 101.3 %copy-start.2 = (s32[512,512]{1,0:T(8,128)S(1)}, s32[512,512]{1,0:T(8,128)}, u32[]{:S(2)}) copy-start(s32[512,512]{1,0:T(8,128)} %param.5) | copy-start | bytes 3145732
  60.2 162.3 %all-gather.5.cloned.1.call-start = ((), (), s32[]{:S(2)}) async-start(), calls=%async_computation.2 | async-start | bytes 4456448 | tf_op jit(solution)/shard_map/all_gather | solution.py:43
  162.5 5.6 %collective-permute-start = (bf16[512,64]{1,0:T(8,128)(2,1)S(1)}, bf16[512,64]{1,0:T(8,128)(2,1)S(1)}, u32[]{:S(2)}, u32[]{:S(2)}) collective-permute-start(bf16[512,64]{1,0:T(8,128)(2,1)S(1)} %fusion.25), channel_id=1, source_target_pairs={{0,1},{1,2},{2,3},{3,4},{4,5},{5,6},{6,7},{7,8},{8,9},{9,10},{10,1... | collective-permute-start | bytes 196616 | tf_op jit(solution)/shard_map/ppermute | solution.py:35
  162.5 5.6 %collective-permute-start.8 = (bf16[512,64]{1,0:T(8,128)(2,1)S(1)}, bf16[512,64]{1,0:T(8,128)(2,1)S(1)}, u32[]{:S(2)}, u32[]{:S(2)}) collective-permute-start(bf16[512,64]{1,0:T(8,128)(2,1)S(1)} %fusion.25), channel_id=1, source_target_pairs={{0,15},{1,0},{2,1},{3,2},{4,3},{5,4},{6,5},{7,6},{8,7},{9,8},{10,9... | collective-permute-start | bytes 196616 | tf_op jit(solution)/shard_map/ppermute | solution.py:38
  168.1 5.6 %collective-permute-start.1 = (bf16[512,64]{1,0:T(8,128)(2,1)S(1)}, bf16[512,64]{1,0:T(8,128)(2,1)S(1)}, u32[]{:S(2)}, u32[]{:S(2)}) collective-permute-start(bf16[512,64]{1,0:T(8,128)(2,1)S(1)} %collective-permute-done), channel_id=1, source_target_pairs={{0,1},{1,2},{2,3},{3,4},{4,5},{5,6},{6,7},{7,8},{8,9},{9,10},{10,1... | collective-permute-start | bytes 196616 | tf_op jit(solution)/shard_map/ppermute | solution.py:35
  168.1 7.6 %collective-permute-start.9 = (bf16[512,64]{1,0:T(8,128)(2,1)S(1)}, bf16[512,64]{1,0:T(8,128)(2,1)S(1)}, u32[]{:S(2)}, u32[]{:S(2)}) collective-permute-start(bf16[512,64]{1,0:T(8,128)(2,1)S(1)} %collective-permute-done.8), channel_id=1, source_target_pairs={{0,15},{1,0},{2,1},{3,2},{4,3},{5,4},{6,5},{7,6},{8,7},{9,8},{10,9... | collective-permute-start | bytes 196616 | tf_op jit(solution)/shard_map/ppermute | solution.py:38
  173.7 7.7 %collective-permute-start.2 = (bf16[512,64]{1,0:T(8,128)(2,1)S(1)}, bf16[512,64]{1,0:T(8,128)(2,1)S(1)}, u32[]{:S(2)}, u32[]{:S(2)}) collective-permute-start(bf16[512,64]{1,0:T(8,128)(2,1)S(1)} %collective-permute-done.1), channel_id=1, source_target_pairs={{0,1},{1,2},{2,3},{3,4},{4,5},{5,6},{6,7},{7,8},{8,9},{9,10},{10,1... | collective-permute-start | bytes 196616 | tf_op jit(solution)/shard_map/ppermute | solution.py:35
  175.8 5.6 %copy-start.5 = (bf16[512,64]{1,0:T(8,128)(2,1)}, bf16[512,64]{1,0:T(8,128)(2,1)S(1)}, u32[]{:S(2)}) copy-start(bf16[512,64]{1,0:T(8,128)(2,1)S(1)} %collective-permute-done.9) | copy-start | bytes 196612
  175.8 8.4 %collective-permute-start.10 = (bf16[512,64]{1,0:T(8,128)(2,1)S(1)}, bf16[512,64]{1,0:T(8,128)(2,1)S(1)}, u32[]{:S(2)}, u32[]{:S(2)}) collective-permute-start(bf16[512,64]{1,0:T(8,128)(2,1)S(1)} %collective-permute-done.9), channel_id=1, source_target_pairs={{0,15},{1,0},{2,1},{3,2},{4,3},{5,4},{6,5},{7,6},{8,7},{9,8},{10,9... | collective-permute-start | bytes 196616 | tf_op jit(solution)/shard_map/ppermute | solution.py:38
  181.4 6.8 %collective-permute-start.3 = (bf16[512,64]{1,0:T(8,128)(2,1)S(1)}, bf16[512,64]{1,0:T(8,128)(2,1)S(1)}, u32[]{:S(2)}, u32[]{:S(2)}) collective-permute-start(bf16[512,64]{1,0:T(8,128)(2,1)S(1)} %collective-permute-done.2), channel_id=1, source_target_pairs={{0,1},{1,2},{2,3},{3,4},{4,5},{5,6},{6,7},{7,8},{8,9},{9,10},{10,1... | collective-permute-start | bytes 196616 | tf_op jit(solution)/shard_map/ppermute | solution.py:35
  184.2 8.7 %collective-permute-start.11 = (bf16[512,64]{1,0:T(8,128)(2,1)S(1)}, bf16[512,64]{1,0:T(8,128)(2,1)S(1)}, u32[]{:S(2)}, u32[]{:S(2)}) collective-permute-start(bf16[512,64]{1,0:T(8,128)(2,1)S(1)} %collective-permute-done.10), channel_id=1, source_target_pairs={{0,15},{1,0},{2,1},{3,2},{4,3},{5,4},{6,5},{7,6},{8,7},{9,8},{10,9... | collective-permute-start | bytes 196616 | tf_op jit(solution)/shard_map/ppermute | solution.py:38
  188.2 4.7 %copy-start.8 = (bf16[512,64]{1,0:T(8,128)(2,1)}, bf16[512,64]{1,0:T(8,128)(2,1)S(1)}, u32[]{:S(2)}) copy-start(bf16[512,64]{1,0:T(8,128)(2,1)S(1)} %collective-permute-done.3) | copy-start | bytes 196612
  188.2 8.2 %collective-permute-start.4 = (bf16[512,64]{1,0:T(8,128)(2,1)S(1)}, bf16[512,64]{1,0:T(8,128)(2,1)S(1)}, u32[]{:S(2)}, u32[]{:S(2)}) collective-permute-start(bf16[512,64]{1,0:T(8,128)(2,1)S(1)} %collective-permute-done.3), channel_id=1, source_target_pairs={{0,1},{1,2},{2,3},{3,4},{4,5},{5,6},{6,7},{7,8},{8,9},{9,10},{10,1... | collective-permute-start | bytes 196616 | tf_op jit(solution)/shard_map/ppermute | solution.py:35
  192.9 8.5 %collective-permute-start.12 = (bf16[512,64]{1,0:T(8,128)(2,1)S(1)}, bf16[512,64]{1,0:T(8,128)(2,1)S(1)}, u32[]{:S(2)}, u32[]{:S(2)}) collective-permute-start(bf16[512,64]{1,0:T(8,128)(2,1)S(1)} %collective-permute-done.11), channel_id=1, source_target_pairs={{0,15},{1,0},{2,1},{3,2},{4,3},{5,4},{6,5},{7,6},{8,7},{9,8},{10,9... | collective-permute-start | bytes 196616 | tf_op jit(solution)/shard_map/ppermute | solution.py:38
  196.4 5.0 %copy-start.10 = (bf16[512,64]{1,0:T(8,128)(2,1)}, bf16[512,64]{1,0:T(8,128)(2,1)S(1)}, u32[]{:S(2)}) copy-start(bf16[512,64]{1,0:T(8,128)(2,1)S(1)} %collective-permute-done.4) | copy-start | bytes 196612
  196.4 8.5 %collective-permute-start.5 = (bf16[512,64]{1,0:T(8,128)(2,1)S(1)}, bf16[512,64]{1,0:T(8,128)(2,1)S(1)}, u32[]{:S(2)}, u32[]{:S(2)}) collective-permute-start(bf16[512,64]{1,0:T(8,128)(2,1)S(1)} %collective-permute-done.4), channel_id=1, source_target_pairs={{0,1},{1,2},{2,3},{3,4},{4,5},{5,6},{6,7},{7,8},{8,9},{9,10},{10,1... | collective-permute-start | bytes 196616 | tf_op jit(solution)/shard_map/ppermute | solution.py:35
  201.4 6.0 %collective-permute-start.13 = (bf16[512,64]{1,0:T(8,128)(2,1)S(1)}, bf16[512,64]{1,0:T(8,128)(2,1)S(1)}, u32[]{:S(2)}, u32[]{:S(2)}) collective-permute-start(bf16[512,64]{1,0:T(8,128)(2,1)S(1)} %collective-permute-done.12), channel_id=1, source_target_pairs={{0,15},{1,0},{2,1},{3,2},{4,3},{5,4},{6,5},{7,6},{8,7},{9,8},{10,9... | collective-permute-start | bytes 196616 | tf_op jit(solution)/shard_map/ppermute | solution.py:38
  204.9 5.6 %collective-permute-start.6 = (bf16[512,64]{1,0:T(8,128)(2,1)S(1)}, bf16[512,64]{1,0:T(8,128)(2,1)S(1)}, u32[]{:S(2)}, u32[]{:S(2)}) collective-permute-start(bf16[512,64]{1,0:T(8,128)(2,1)S(1)} %collective-permute-done.5), channel_id=1, source_target_pairs={{0,1},{1,2},{2,3},{3,4},{4,5},{5,6},{6,7},{7,8},{8,9},{9,10},{10,1... | collective-permute-start | bytes 196616 | tf_op jit(solution)/shard_map/ppermute | solution.py:35
  207.4 5.6 %copy-start.13 = (bf16[512,64]{1,0:T(8,128)(2,1)}, bf16[512,64]{1,0:T(8,128)(2,1)S(1)}, u32[]{:S(2)}) copy-start(bf16[512,64]{1,0:T(8,128)(2,1)S(1)} %collective-permute-done.13) | copy-start | bytes 196612
  207.4 5.6 %collective-permute-start.14 = (bf16[512,64]{1,0:T(8,128)(2,1)S(1)}, bf16[512,64]{1,0:T(8,128)(2,1)S(1)}, u32[]{:S(2)}, u32[]{:S(2)}) collective-permute-start(bf16[512,64]{1,0:T(8,128)(2,1)S(1)} %collective-permute-done.13), channel_id=1, source_target_pairs={{0,15},{1,0},{2,1},{3,2},{4,3},{5,4},{6,5},{7,6},{8,7},{9,8},{10,9... | collective-permute-start | bytes 196616 | tf_op jit(solution)/shard_map/ppermute | solution.py:38
  210.5 5.7 %collective-permute-start.7 = (bf16[512,64]{1,0:T(8,128)(2,1)S(1)}, bf16[512,64]{1,0:T(8,128)(2,1)}, u32[]{:S(2)}, u32[]{:S(2)}) collective-permute-start(bf16[512,64]{1,0:T(8,128)(2,1)S(1)} %collective-permute-done.6), channel_id=1, source_target_pairs={{0,1},{1,2},{2,3},{3,4},{4,5},{5,6},{6,7},{7,8},{8,9},{9,10},{10,1... | collective-permute-start | bytes 196616 | tf_op jit(solution)/shard_map/ppermute | solution.py:35
  (11 other events, 26.6 us)
Sparse Core Ops, SparseCore 0:
  9.2 45.0 all-gather.2
  60.3 98.6 all-reduce.1
  161.7 44.6 all-gather.4
